TPU v7x, 32 devices: a whole 2x2x4 slice. The times are simulated.
32 devices in a mesh: groups: 2 (over y), block: 4 (over x, core), tile: 4 (over z).
Axes of the slice: x: 2, y: 2, z: 4, core: 2. Of those that a mesh axis runs over, the one named last changes fastest.
Arguments:
- queries: float32 [8, 4, 16, 24, 1024], P(('groups', 'block'), 'tile'), parts along dimension 0
- keys: float32 [8, 4, 16, 24, 1024], P(('groups', 'block'), 'tile'), parts along dimension 0
- values: float32 [8, 4, 16, 24, 1024], P(('groups', 'block'), 'tile'), parts along dimension 0, may hold values from -6 to 6
- radii: int32 [4], replicated, may hold values from 1 to 4, as said below
Outputs:
- local_out: float32 [8, 4, 16, 24, 1024], P(('groups', 'block'), 'tile'), parts along dimension 0
- global_out: float32 [8, 4, 16, 24, 1024], P(('groups', 'block'), 'tile'), parts along dimension 0
There are 2 independent parts, one for each index of `groups`. A program takes and returns all parts, laid end to end along the dimension named above; an argument that names none is the same for every part. Nothing has to cross between parts.
Inputs may be any that keep to these rules, and one draw needn't show every extreme that they name: `radii`: every head's radius is at least 1 and some head has radius 4.
All inputs are finite; a program needn't handle non-finite values.
Results may differ from a plain program's by a relative error of at most 0.0003.
Values sent between devices are 32-bit elements; how exact they have to be, the bound alone decides.
No kernel may reach another device: no remote copies, remote signals or barrier semaphores. Data moves between devices by JAX's collectives and lax.ppermute only.
A program may use at most 128 MiB of HBM per device.

v0:
```python
import math

import jax
import jax.numpy as jnp
from jax import lax
from jax.sharding import PartitionSpec as P

R_MAX = 4


def from_behind(value, axis, steps):
    count = lax.axis_size(axis)
    pairs = [(source, (source + steps) % count) for source in range(count)]
    return lax.ppermute(value, axis, pairs)


def entering(shard, axis, combine, identity):
    devices, mine = (lax.axis_size(axis), lax.axis_index(axis))
    everything = jax.tree.map(lambda part: lax.all_gather(part, axis), shard)
    start = jax.tree.map(
        lambda part, zero: jnp.broadcast_to(jnp.asarray(zero, part.dtype), part.shape),
        shard,
        identity,
    )

    def turn(k, before):
        reached = k < mine
        new = combine(before, jax.tree.map(lambda part: part[k], everything))
        return jax.tree.map(lambda a, b: jnp.where(reached, a, b), new, before)

    return lax.fori_loop(0, devices, turn, start)


def neighborhood(query_tile, key_tile, value_tile, radii, row_start, col_start, height, width):
    rows, cols, dim = query_tile.shape
    head_count = radii.shape[0]
    head_dim = dim // head_count
    key_h = key_tile.shape[0]
    key_w = key_tile.shape[1]
    row_margin = (key_h - rows) // 2
    col_margin = (key_w - cols) // 2
    query_rows = query_tile.reshape(rows * cols, head_count, head_dim)
    key_rows = key_tile.reshape(key_h * key_w, head_count, head_dim)
    value_rows = value_tile.reshape(key_h * key_w, head_count, head_dim)
    scores = jnp.einsum(
        "qhd,khd->hqk", query_rows, key_rows, precision=lax.Precision.HIGHEST
    ) / math.sqrt(head_dim)
    query_pos = jnp.arange(rows * cols, dtype=jnp.int32)
    key_pos = jnp.arange(key_h * key_w, dtype=jnp.int32)
    query_row = query_pos // cols
    query_col = query_pos % cols
    key_row = key_pos // key_w - row_margin
    key_col = key_pos % key_w - col_margin
    reach = jnp.maximum(
        jnp.abs(query_row[:, None] - key_row[None, :]),
        jnp.abs(query_col[:, None] - key_col[None, :]),
    )
    inside = (
        (col_start + key_col >= 0)
        & (col_start + key_col < width)
        & (row_start + key_row >= 0)
        & (row_start + key_row < height)
    )
    allowed = (reach[None, :, :] <= radii[:, None, None]) & inside[None, None, :]
    scores = jnp.where(allowed, scores, jnp.float32(-1e30))
    top = jnp.max(scores, axis=-1, keepdims=True)
    weights = jnp.exp(scores - top)
    weights = weights / jnp.sum(weights, axis=-1, keepdims=True)
    result = jnp.einsum("hqk,khd->qhd", weights, value_rows, precision=lax.Precision.HIGHEST)
    return result.reshape(rows, cols, dim)


def add_states(earlier, later):
    return jax.tree.map(lambda left, right: left + right, earlier, later)


def body(queries, keys, values, radii):
    rows, cols, dim = (queries.shape[2], queries.shape[3], queries.shape[4])
    head_count = radii.shape[0]
    head_dim = dim // head_count
    tile_count = lax.axis_size("tile")
    grid_cols = min(4, tile_count // 2)
    grid_rows = tile_count // grid_cols
    height = grid_rows * rows
    width = grid_cols * cols
    tile_here = lax.axis_index("tile")
    position = (tile_here + 1) % tile_count
    row_start = position // grid_cols * rows
    col_start = position % grid_cols * cols
    stacked = jnp.stack([keys[0, 0], values[0, 0]])
    side_parts = [
        from_behind(piece, "tile", by_step)
        for by_step, piece in ((1, stacked[:, :, cols - R_MAX :]), (-1, stacked[:, :, :R_MAX]))
    ]
    widened = jnp.concatenate([side_parts[0], stacked, side_parts[1]], axis=2)
    edge_parts = [
        from_behind(piece, "tile", by_step)
        for by_step, piece in (
            (grid_cols, widened[:, rows - R_MAX :]),
            (-grid_cols, widened[:, :R_MAX]),
        )
    ]
    padded = jnp.concatenate([edge_parts[0], widened, edge_parts[1]], axis=1)
    local_tile = neighborhood(
        queries[0, 0], padded[0], padded[1], radii, row_start, col_start, height, width
    )
    key_rows = keys[0, 0].reshape(rows * cols, head_count, head_dim)
    value_rows = values[0, 0].reshape(rows * cols, head_count, head_dim)
    feature = jax.nn.relu(key_rows)
    state = jnp.einsum("khd,khe->hde", feature, value_rows, precision=lax.Precision.HIGHEST)
    zsum = jnp.sum(feature, axis=0)
    vsum = jnp.sum(value_rows, axis=0)
    own = (state, zsum, vsum)
    zeros = jax.tree.map(jnp.zeros_like, own)
    earlier = entering(own, "block", add_states, zeros)
    full_state, full_z, full_v = lax.psum(add_states(earlier, own), "tile")
    count = ((lax.axis_index("block") + 1) * height * width).astype(jnp.float32)
    query_rows = jax.nn.relu(queries[0, 0].reshape(rows * cols, head_count, head_dim))
    numer = (
        jnp.einsum("qhd,hde->qhe", query_rows, full_state, precision=lax.Precision.HIGHEST)
        / math.sqrt(head_dim)
        + full_v[None, :, :]
    )
    denom = (
        jnp.einsum("qhd,hd->qh", query_rows, full_z, precision=lax.Precision.HIGHEST)
        / math.sqrt(head_dim)
        + count
    )
    global_tile = (numer / denom[:, :, None]).reshape(1, 1, rows, cols, dim)
    return (local_tile.reshape(1, 1, rows, cols, dim), global_tile)


def solution(mesh):
    return jax.shard_map(
        body,
        mesh=mesh,
        in_specs=(
            P(("groups", "block"), "tile", None, None, None),
            P(("groups", "block"), "tile", None, None, None),
            P(("groups", "block"), "tile", None, None, None),
            P(),
        ),
        out_specs=(
            P(("groups", "block"), "tile", None, None, None),
            P(("groups", "block"), "tile", None, None, None),
        ),
        check_vma=False,
    )
```

profile of v0, /device:TPU:17, one launch (start us, length us, event | category | flops | bytes accessed | tf_op | source)
XLA Modules:
  0.0 243.1 jit_solution(8093740516286024459)
XLA Ops:
  7.2 0.0 all-gather.3.cloned.1.call-start
  7.2 1.7 fusion.49
  8.9 0.0 copy-start
  8.9 1.9 max.28
  10.7 1.9 reshape_squeeze.17
  12.6 6.0 %fusion.14 = f32[4,256,256]{2,1,0:T(8,128)} fusion(f32[384,4,256]{2,1,0:T(4,128)} %reshape_squeeze.17, f32[384,4,256]{2,1,0:T(4,128)} %max.28), kind=kOutput, calls=%fused_computation.21 | convolution fusion | flops 1207959552 | bytes 4194304 | tf_op jit(solution)/shard_map/khd,khe->hde/dot_general | solution.py:110
  18.6 0.0 all-gather.3.cloned.1.call-update
  18.6 0.0 all-reduce.3.cloned.1.call-start
  18.7 0.3 pad_maximum_fusion.6
  18.9 1.4 collective-permute-start
  20.3 0.2 collective-permute-start.1
  20.4 11.6 %collective-permute-done = f32[2,16,4,1024]{3,2,1,0:T(4,128)S(1)} collective-permute-done((f32[2,16,4,1024]{3,2,1,0:T(4,128)S(1)}, f32[2,16,4,1024]{3,2,1,0:T(4,128)S(1)}, u32[]{:S(2)}, u32[]{:S(2)}) %collective-permute-start) | collective-permute-done | bytes 524320 | tf_op jit(solution)/shard_map/ppermute | solution.py:14
  32.0 11.3 %collective-permute-done.1 = f32[2,16,4,1024]{3,2,1,0:T(4,128)S(1)} collective-permute-done((f32[2,16,4,1024]{3,2,1,0:T(4,128)S(1)}, f32[2,16,4,1024]{3,2,1,0:T(4,128)S(1)}, u32[]{:S(2)}, u32[]{:S(2)}) %collective-permute-start.1) | collective-permute-done | bytes 524320 | tf_op jit(solution)/shard_map/ppermute | solution.py:14
  43.3 1.8 pad_maximum_fusion.4
  45.1 0.0 copy-done.7
  45.1 1.6 collective-permute-start.2
  46.7 0.7 collective-permute-start.3
  47.5 0.1 reduce_sum.33
  47.6 2.9 %reshape_squeeze.16 = f32[384,4,256]{2,1,0:T(4,128)} reshape(f32[1,1,16,24,1024]{4,3,2,1,0:T(8,128)} %param.6) | data formatting | bytes 3145728 | tf_op jit(solution)/shard_map/reshape;squeeze | solution.py:42
  50.5 7.0 %all_gather.21 = f32[4,4,256]{2,1,0:T(4,128)S(1)} all-gather(f32[1,4,256]{2,1,0:T(4,128)S(1)} %all_gather.20), channel_id=1, replica_groups=mesh['groups'=2,'block'=4,'tile'=4] {'block'}, dimensions={0}, use_global_device_ids=true | all-gather | bytes 20480 | tf_op jit(solution)/shard_map/all_gather | solution.py:19
  57.5 5.4 %all_gather.23 = f32[4,4,256]{2,1,0:T(4,128)S(1)} all-gather(f32[1,4,256]{2,1,0:T(4,128)S(1)} %all_gather.22), channel_id=1, replica_groups=mesh['groups'=2,'block'=4,'tile'=4] {'block'}, dimensions={0}, use_global_device_ids=true | all-gather | bytes 20480 | tf_op jit(solution)/shard_map/all_gather | solution.py:19
  62.9 1.5 abs_maximum_fusion
  64.4 49.3 %collective-permute-done.2 = f32[2,4,32,1024]{3,2,1,0:T(8,128)} collective-permute-done((f32[2,4,32,1024]{3,2,1,0:T(8,128)}, f32[2,4,32,1024]{3,2,1,0:T(8,128)}, u32[]{:S(2)}, u32[]{:S(2)}) %collective-permute-start.2) | collective-permute-done | bytes 1048608 | tf_op jit(solution)/shard_map/ppermute | solution.py:14
  113.7 22.5 %collective-permute-done.3 = f32[2,4,32,1024]{3,2,1,0:T(8,128)} collective-permute-done((f32[2,4,32,1024]{3,2,1,0:T(8,128)}, f32[2,4,32,1024]{3,2,1,0:T(8,128)}, u32[]{:S(2)}, u32[]{:S(2)}) %collective-permute-start.3) | collective-permute-done | bytes 1048608 | tf_op jit(solution)/shard_map/ppermute | solution.py:14
  136.2 2.5 %pad_maximum_fusion = f32[2,24,32,1024]{3,2,1,0:T(8,128)S(1)} fusion(f32[2,4,32,1024]{3,2,1,0:T(8,128)} %collective-permute-done.3, f32[2,16,4,1024]{3,2,1,0:T(4,128)S(1)} %copy-done.8, f32[1,16,24,1024]{3,2,1,0:T(8,128)S(1)} %bitcast.50, f32[1,16,24,1024]{3,2,1,0:T(8,128)} %bitcast.51, f32[2,16,4,1024]{3,2,1,0:T(4,128)S(1)} %copy-done.6, ...), kind=kLoop, calls=%fused_computation.3 | loop fusion | flops 7864320 | bytes 12582912 | tf_op jit(solution)/shard_map/concatenate | solution.py:103
  138.7 3.3 %fusion.50 = (f32[1,24,32,1024]{3,2,1,0:T(8,128)}, f32[1,24,32,1024]{3,2,1,0:T(8,128)}) fusion(f32[2,24,32,1024]{3,2,1,0:T(8,128)S(1)} %pad_maximum_fusion), kind=kLoop, calls=%fused_computation.72 | loop fusion | bytes 12582912 | tf_op jit(solution)/shard_map/slice | solution.py:105
  142.0 5.1 %reshape_squeeze.15 = f32[768,4,256]{2,1,0:T(4,128)} reshape(f32[1,24,32,1024]{3,2,1,0:T(8,128)} %get-tuple-element.196) | data formatting | bytes 6291456 | tf_op jit(solution)/shard_map/reshape;squeeze | solution.py:43
  147.1 5.3 %reshape_squeeze.14 = f32[768,4,256]{2,1,0:T(4,128)} reshape(f32[1,24,32,1024]{3,2,1,0:T(8,128)} %get-tuple-element.195) | data formatting | bytes 6291456 | tf_op jit(solution)/shard_map/reshape;squeeze | solution.py:44
  152.4 8.8 %fusion.6 = (f32[4,384]{1,0:T(4,128)S(1)}, f32[4,768,384]{2,1,0:T(8,128)S(1)}) fusion(s32[384,768]{0,1:T(8,128)} %abs_maximum_fusion, s32[4]{0:T(128)S(1)} %copy-done.9, pred[768]{0:T(1024)(128)(4,1)S(1)} %compare_and_fusion, f32[384,4,256]{2,1,0:T(4,128)S(1)} %copy-done.3, f32[768,4,256]{2,1,0:T(4,128)} %reshape_squeeze.15), kind=kOutput, calls=%fused_computation.12 | convolution fusion | flops 3629775360 | bytes 10623760 | tf_op jit(solution)/shard_map/qhd,khd->hqk/dot_general | solution.py:45
  161.3 2.2 copy-done.1
  163.5 1.9 fusion.2
  165.4 0.0 all-gather.3.cloned.1.call-done
  165.4 6.5 %while.18 = (s32[]{:T(128)}, f32[4,256,256]{2,1,0:T(8,128)S(1)}, f32[4,256]{1,0:T(4,128)S(1)}, f32[4,256]{1,0:T(4,128)S(1)}, s32[]{:T(128)}, /*index=5*/f32[4,4,...) while((s32[]{:T(128)}, f32[4,256,256]{2,1,0:T(8,128)S(1)}, ...), condition=%wide.region_5.6_spmd.clone, body=%wide.region_4.5_spmd.clone.sunk | while | flops 792580 | bytes 3170435 | solution.py:31
  165.5 1.6 add_select_fusion.7
  167.1 1.6 add_select_fusion.7
  168.7 1.6 add_select_fusion.7
  170.3 1.6 add_select_fusion.7
  171.9 2.3 add.184
  174.2 0.0 all-reduce.3.cloned.1.call-update
  174.3 14.4 %fusion.17 = f32[384,4,256]{0,2,1:T(8,128)} fusion(f32[4,768,384]{2,1,0:T(8,128)} %copy-done.1, f32[4,384]{1,0:T(4,128)S(1)} %fusion.2, f32[4,384]{1,0:T(4,128)S(1)} %get-tuple-element.203, s32[384,768]{0,1:T(8,128)} %abs_maximum_fusion, s32[4]{0:T(128)S(1)} %copy-done.9, pred[768]{0:T(1024)(128)(4,1)S(1)} %compare_and_fusion, ...), kind=kOutput, calls=%fused_computation.24 | convolution fusion | flops 3630956544 | bytes 10629904 | tf_op jit(solution)/shard_map/hqk,khd->qhd/dot_general | solution.py:69
  188.6 1.9 copy.29
  190.5 2.0 reshape_reshape.3
  192.5 9.9 %all-reduce = (f32[4,256]{1,0:T(4,128)S(1)}, f32[4,256]{1,0:T(4,128)S(1)}) all-reduce(f32[4,256]{1,0:T(4,128)S(1)} %add.189, f32[4,256]{1,0:T(4,128)S(1)} %add.185), channel_id=1, replica_groups=mesh['groups'=2,'block'=4,'tile'=4] {'tile'}, use_global_device_ids=true, to_apply=%region_8.9 | all-reduce | flops 2048 | bytes 16384 | tf_op jit(solution)/shard_map/psum | solution.py:116
  202.4 1.5 fusion.23
  203.9 24.6 %all-reduce.3.cloned.1.call-done = f32[4,256,256]{2,1,0:T(8,128)} async-done(((f32[4,256,256]{2,1,0:T(8,128)}), f32[4,256,256]{2,1,0:T(8,128)}) %all-reduce.3.cloned.1.call-update) | async-done | bytes 1048592 | tf_op jit(solution)/shard_map/psum | solution.py:116
  228.5 4.8 %bitcast_divide_fusion = f32[384,4,256]{0,2,1:T(8,128)S(1)} fusion(f32[4,256,256]{2,1,0:T(8,128)} %all-reduce.3.cloned.1.call-done, f32[384,4,256]{2,1,0:T(4,128)S(1)} %copy-done.3, f32[384,4]{0,1:T(4,128)S(1)} %fusion.31, f32[4,256]{1,0:T(4,128)S(1)} %get-tuple-element.192), kind=kOutput, calls=%fused_computation.20 | convolution fusion | flops 1209532416 | bytes 4204544 | tf_op jit(solution)/shard_map/qhd,hde->qhe/dot_general | solution.py:120
  233.4 0.9 copy.34
  234.3 2.0 reshape.149
  (34 shorter events, 0.2 us)
Async XLA Ops:
  7.2 158.3 %all-gather.3.cloned.1.call-start = ((), (), s32[]{:S(2)}) async-start(), calls=%async_computation.1 | async-start | bytes 5242880 | tf_op jit(solution)/shard_map/all_gather | solution.py:19
  8.9 1.9 copy-start
  12.6 6.1 %copy-start.2 = (f32[1,1,16,24,1024]{4,3,2,1,0:T(8,128)S(1)}, f32[1,1,16,24,1024]{4,3,2,1,0:T(8,128)}, u32[]{:S(2)}) copy-start(f32[1,1,16,24,1024]{4,3,2,1,0:T(8,128)} %param.7) | copy-start | bytes 4718596
  18.6 209.9 %all-reduce.3.cloned.1.call-start = ((), (), s32[]{:S(2)}) async-start(), calls=%async_computation | async-start | bytes 2097152 | tf_op jit(solution)/shard_map/psum | solution.py:116
  18.9 13.1 %collective-permute-start = (f32[2,16,4,1024]{3,2,1,0:T(4,128)S(1)}, f32[2,16,4,1024]{3,2,1,0:T(4,128)S(1)}, u32[]{:S(2)}, u32[]{:S(2)}) collective-permute-start(f32[2,16,4,1024]{3,2,1,0:T(4,128)S(1)} %get-tuple-element.199), channel_id=1, source_target_pairs={{0,1},{1,2},{2,3},{3,0},{4,5},{5,6},{6,7},{7,4},{8,9},{9,10},{10,1... | collective-permute-start | bytes 1572872 | tf_op jit(solution)/shard_map/ppermute | solution.py:14
  20.3 23.0 %collective-permute-start.1 = (f32[2,16,4,1024]{3,2,1,0:T(4,128)S(1)}, f32[2,16,4,1024]{3,2,1,0:T(4,128)S(1)}, u32[]{:S(2)}, u32[]{:S(2)}) collective-permute-start(f32[2,16,4,1024]{3,2,1,0:T(4,128)S(1)} %get-tuple-element.200), channel_id=1, source_target_pairs={{0,3},{1,0},{2,1},{3,2},{4,7},{5,4},{6,5},{7,6},{8,11},{9,8},{10,9... | collective-permute-start | bytes 1572872 | tf_op jit(solution)/shard_map/ppermute | solution.py:14
  32.0 13.1 %copy-start.5 = (f32[2,16,4,1024]{3,2,1,0:T(4,128)}, f32[2,16,4,1024]{3,2,1,0:T(4,128)S(1)}, u32[]{:S(2)}) copy-start(f32[2,16,4,1024]{3,2,1,0:T(4,128)S(1)} %collective-permute-done) | copy-start | bytes 1572868
  43.3 1.8 copy-start.7
  45.1 68.6 %collective-permute-start.2 = (f32[2,4,32,1024]{3,2,1,0:T(8,128)}, f32[2,4,32,1024]{3,2,1,0:T(8,128)}, u32[]{:S(2)}, u32[]{:S(2)}) collective-permute-start(f32[2,4,32,1024]{3,2,1,0:T(8,128)} %get-tuple-element.197), channel_id=1, source_target_pairs={{0,2},{1,3},{2,0},{3,1},{4,6},{5,7},{6,4},{7,5},{8,10},{9,11},{10,... | collective-permute-start | bytes 3145736 | tf_op jit(solution)/shard_map/ppermute | solution.py:14
  46.7 89.5 %collective-permute-start.3 = (f32[2,4,32,1024]{3,2,1,0:T(8,128)}, f32[2,4,32,1024]{3,2,1,0:T(8,128)}, u32[]{:S(2)}, u32[]{:S(2)}) collective-permute-start(f32[2,4,32,1024]{3,2,1,0:T(8,128)} %get-tuple-element.198), channel_id=1, source_target_pairs={{0,2},{1,3},{2,0},{3,1},{4,6},{5,7},{6,4},{7,5},{8,10},{9,11},{10,... | collective-permute-start | bytes 3145736 | tf_op jit(solution)/shard_map/ppermute | solution.py:14
  47.6 88.6 %copy-start.6 = (f32[2,16,4,1024]{3,2,1,0:T(4,128)S(1)}, f32[2,16,4,1024]{3,2,1,0:T(4,128)}, u32[]{:S(2)}) copy-start(f32[2,16,4,1024]{3,2,1,0:T(4,128)} %copy-done.5) | copy-start | bytes 1572868
  50.5 85.6 %copy-start.8 = (f32[2,16,4,1024]{3,2,1,0:T(4,128)S(1)}, f32[2,16,4,1024]{3,2,1,0:T(4,128)}, u32[]{:S(2)}) copy-start(f32[2,16,4,1024]{3,2,1,0:T(4,128)} %copy-done.7) | copy-start | bytes 1572868
  147.1 5.3 %copy-start.3 = (f32[384,4,256]{2,1,0:T(4,128)S(1)}, f32[384,4,256]{2,1,0:T(4,128)}, u32[]{:S(2)}) copy-start(f32[384,4,256]{2,1,0:T(4,128)} %reshape_squeeze.16) | copy-start | bytes 4718596
  147.1 5.3 %copy-start.9 = (s32[4]{0:T(128)S(1)}, s32[4]{0:T(128)}, u32[]{:S(2)}) copy-start(s32[4]{0:T(128)} %param.9) | copy-start | bytes 52
  152.4 11.1 %copy-start.4 = (s32[384,768]{0,1:T(8,128)S(1)}, s32[384,768]{0,1:T(8,128)}, u32[]{:S(2)}) copy-start(s32[384,768]{0,1:T(8,128)} %abs_maximum_fusion) | copy-start | bytes 3538948
  161.3 2.2 copy-start.1
Sparse Core Ops, SparseCore 0:
  18.7 35.9 all-gather.2
  174.4 54.0 all-reduce.2
where the time goes:
time: 246 us; the launch traced here: 243 us
  waiting for transfers between devices  119 us (48%)
  matrix products  35.6 us (14%)
  local copies, waits for them, and re-layouts  29.3 us (12%)
  blocking collectives  22.2 us (9%)
  other arithmetic  18.4 us (7%)
  between operations  14.2 us (6%)
  starting transfers between devices  3.96 us (2%)
    ppermute x4, waiting for transfers between devices, from_behind(): return lax.ppermute(value, axis, pairs)  94.6 us
    psum x1, waiting for transfers between devices, body(): full_state, full_z, full_v = lax.psum(add_states(earlier, own), 'tile')  24.6 us
    dot_general x1, matrix products, neighborhood(): jnp.einsum('hqk,khd->qhd', weights, value_rows, precision=lax.Precision.H...  14.4 us
    all_gather x2, blocking collectives, entering(): everything = jax.tree.map(lambda part: lax.all_gather(part, axis), shard)  12.3 us
    psum x1, blocking collectives, body(): full_state, full_z, full_v = lax.psum(add_states(earlier, own), 'tile')  9.89 us
    dot_general x1, matrix products, neighborhood(): jnp.einsum('qhd,khd->hqk', query_rows, key_rows, precision=lax.Precision....  8.85 us
    select_n x8, other arithmetic, turn(): return jax.tree.map(lambda a, b: jnp.where(reached, a, b), new, before)  6.36 us
    dot_general x1, matrix products, body(): jnp.einsum('khd,khe->hde', feature, value_rows, precision=lax.Precision.H...  5.98 us
  transfers between devices with their start and end apart: 6, of which 5 were waited for; matrix products, arithmetic and copies ran while one was open for 22% of the time, Pallas kernels for 0%

commit v1 on v0

v1 whole, which is shorter than its diff:
```python
import functools
import math

import jax
import jax.numpy as jnp
from jax import lax
from jax.experimental import pallas as pl
from jax.experimental.pallas import tpu as pltpu
from jax.sharding import PartitionSpec as P

R_MAX = 4
SUB = 8
EXACT = lax.Precision.HIGHEST
VMEM_LIMIT = 48 * 1024 * 1024


class Grid:
    def __init__(self, tiles, blocks):
        self.tiles = tiles
        self.blocks = blocks
        self.cols = min(4, tiles // 2)
        self.rows = tiles // self.cols
        self.col_sides = self.sides(self.cols)
        self.row_sides = self.sides(self.rows)

    @staticmethod
    def sides(count):
        return {1: (), 2: (0,)}.get(count, (-1, 1))

    @staticmethod
    def moved(place, side, count):
        if side == 0:
            return 1 - place
        there = place + side
        return there if 0 <= there < count else None

    def pairs(self, row_side, col_side):
        found = []
        for place in range(self.tiles):
            row, col = divmod(place, self.cols)
            if row_side is not None:
                row = self.moved(row, row_side, self.rows)
            if col_side is not None:
                col = self.moved(col, col_side, self.cols)
            if row is None or col is None:
                continue
            source = row * self.cols + col
            found.append(((source - 1) % self.tiles, (place - 1) % self.tiles))
        return found

    def place(self, tile):
        spot = lax.rem(tile + 1, self.tiles)
        return lax.div(spot, self.cols), lax.rem(spot, self.cols)

    @staticmethod
    def sends_high(place, side):
        return (place == 0) if side == 0 else (side == -1)

    @staticmethod
    def lies_after(place, side):
        return (place == 0) if side == 0 else (side == 1)

    @staticmethod
    def exists(place, side, count):
        if side == 0:
            return True
        return (place > 0) if side == -1 else (place < count - 1)


def pick(flag, yes, no):
    if isinstance(flag, bool):
        return yes if flag else no
    return jnp.where(flag, yes, no)


def whole(shape):
    return pl.BlockSpec(shape, lambda *_: (0,) * len(shape))


def pack_kernel(grid, heads, tile_ref, *refs):
    n_col, n_row = len(grid.col_sides), len(grid.row_sides)
    col_in = refs[: 2 * n_col]
    row_in = refs[2 * n_col : 2 * (n_col + n_row)]
    out = list(refs[2 * (n_col + n_row) :])
    row, col = grid.place(tile_ref[0])
    dim = (col_in + row_in)[0].shape[-1]
    head_dim = dim // heads
    for i, side in enumerate(grid.col_sides):
        high = grid.sends_high(col, side)
        target = out.pop(0)
        for kind in range(2):
            source = col_in[2 * i + kind].at[0, 0]
            for level in range(1, R_MAX + 1):
                line = pick(high, source[:, SUB - level, :], source[:, level - 1, :])
                for head in range(heads):
                    target[head * R_MAX + level - 1, kind] = line[
                        :, head * head_dim : (head + 1) * head_dim
                    ]
    for i, side in enumerate(grid.row_sides):
        high = grid.sends_high(row, side)
        target = out.pop(0)
        for kind in range(2):
            source = row_in[2 * i + kind].at[0, 0]
            for level in range(1, R_MAX + 1):
                at = pick(high, R_MAX - level, level - 1)
                line = source[at]
                for head in range(heads):
                    target[head * R_MAX + level - 1, kind] = line[
                        :, head * head_dim : (head + 1) * head_dim
                    ]
    for i, _ in enumerate(grid.row_sides):
        for side in grid.col_sides:
            high = grid.sends_high(col, side)
            target = out.pop(0)
            for kind in range(2):
                source = row_in[2 * i + kind].at[0, 0]
                cols = source.shape[1]
                for a in range(R_MAX):
                    target[kind, a * R_MAX : (a + 1) * R_MAX, :] = pick(
                        high, source[a, cols - R_MAX :, :], source[a, :R_MAX, :]
                    )


def pack(grid, tile, keys, values, heads):
    rows, cols, dim = keys.shape[2:]
    head_dim = dim // heads
    units = heads * R_MAX

    def col_map(side):
        def index(_, tile_ref):
            high = grid.sends_high(grid.place(tile_ref[0])[1], side)
            return (0, 0, 0, pick(high, cols // SUB - 1, 0), 0)

        return index

    def row_map(side):
        def index(_, tile_ref):
            high = grid.sends_high(grid.place(tile_ref[0])[0], side)
            return (0, 0, pick(high, rows // R_MAX - 1, 0), 0, 0)

        return index

    in_specs, operands, shapes = [], [], []
    for side in grid.col_sides:
        for array in (keys, values):
            in_specs.append(pl.BlockSpec((1, 1, rows, SUB, dim), col_map(side)))
            operands.append(array)
        shapes.append((units, 2, rows, head_dim))
    for side in grid.row_sides:
        for array in (keys, values):
            in_specs.append(pl.BlockSpec((1, 1, R_MAX, cols, dim), row_map(side)))
            operands.append(array)
        shapes.append((units, 2, cols, head_dim))
    for _ in grid.row_sides:
        for _ in grid.col_sides:
            shapes.append((2, R_MAX * R_MAX, dim))
    return pl.pallas_call(
        functools.partial(pack_kernel, grid, heads),
        name="pack_edges",
        out_shape=[jax.ShapeDtypeStruct(shape, jnp.float32) for shape in shapes],
        grid_spec=pltpu.PrefetchScalarGridSpec(
            num_scalar_prefetch=1,
            grid=(1,),
            in_specs=in_specs,
            out_specs=[whole(shape) for shape in shapes],
        ),
        compiler_params=pltpu.CompilerParams(vmem_limit_bytes=VMEM_LIMIT),
        cost_estimate=pl.CostEstimate(flops=0, transcendentals=0, bytes_accessed=6 << 20),
    )(tile, *operands)


def state_kernel(base_ref, key_ref, value_ref, out_ref):
    rows, cols, head_dim = key_ref.shape[2:]
    feature = jnp.maximum(key_ref[0, 0].reshape(rows * cols, head_dim), 0.0)
    value = value_ref[0, 0].reshape(rows * cols, head_dim)
    out_ref[0, :head_dim, :] = lax.dot_general(
        feature, value, (((0,), (0,)), ((), ())), precision=EXACT,
        preferred_element_type=jnp.float32,
    )
    line = lax.broadcasted_iota(jnp.int32, (SUB, head_dim), 0)
    vsum = jnp.sum(value, axis=0, keepdims=True)
    zsum = jnp.sum(feature, axis=0, keepdims=True)
    out_ref[0, head_dim:, :] = jnp.where(
        line == 0, vsum, jnp.where(line == 1, zsum, 0.0)
    )


def states(base, keys, values, heads, count):
    rows, cols, dim = keys.shape[2:]
    head_dim = dim // heads
    part = pl.BlockSpec(
        (1, 1, rows, cols, head_dim), lambda i, base_ref: (0, 0, 0, 0, base_ref[0] + i)
    )
    return pl.pallas_call(
        state_kernel,
        name="head_states",
        out_shape=jax.ShapeDtypeStruct((count, head_dim + SUB, head_dim), jnp.float32),
        grid_spec=pltpu.PrefetchScalarGridSpec(
            num_scalar_prefetch=1,
            grid=(count,),
            in_specs=[part, part],
            out_specs=pl.BlockSpec(
                (1, head_dim + SUB, head_dim), lambda i, base_ref: (i, 0, 0)
            ),
        ),
        compiler_params=pltpu.CompilerParams(vmem_limit_bytes=VMEM_LIMIT),
        cost_estimate=pl.CostEstimate(
            flops=count * 12 * rows * cols * head_dim * head_dim,
            transcendentals=0,
            bytes_accessed=count * 8 * rows * cols * head_dim,
        ),
    )(base, keys, values)


def global_kernel(tokens, aliased, base_ref, block_ref, query_ref, state_ref, *refs):
    out_ref = refs[-1]
    rows, cols, head_dim = query_ref.shape[2:]
    query = jnp.maximum(query_ref[0, 0].reshape(rows * cols, head_dim), 0.0)
    root = math.sqrt(head_dim)
    count = ((block_ref[0] + 1) * tokens).astype(jnp.float32)
    numer = (
        jnp.dot(
            query, state_ref[0, :head_dim, :], precision=EXACT,
            preferred_element_type=jnp.float32,
        )
        / root
        + state_ref[0, head_dim : head_dim + 1, :]
    )
    zsum = state_ref[0, head_dim + 1 : head_dim + 2, :]
    denom = jnp.sum(query * zsum, axis=1, keepdims=True) / root + count
    out_ref[0, 0] = (numer / denom).reshape(rows, cols, head_dim)


def global_part(base, block, queries, state, tokens, heads, onto=None):
    rows, cols, dim = queries.shape[2:]
    head_dim = dim // heads
    count = state.shape[0]
    part = pl.BlockSpec(
        (1, 1, rows, cols, head_dim),
        lambda i, base_ref, block_ref: (0, 0, 0, 0, base_ref[0] + i),
    )
    operands = [queries, state]
    in_specs = [
        part,
        pl.BlockSpec((1, head_dim + SUB, head_dim), lambda i, *_: (i, 0, 0)),
    ]
    aliases = {}
    if onto is not None:
        operands.append(onto)
        in_specs.append(pl.BlockSpec(memory_space=pl.ANY))
        aliases = {4: 0}
    return pl.pallas_call(
        functools.partial(global_kernel, tokens, onto is not None),
        name="global_heads",
        out_shape=jax.ShapeDtypeStruct(queries.shape, jnp.float32),
        grid_spec=pltpu.PrefetchScalarGridSpec(
            num_scalar_prefetch=2, grid=(count,), in_specs=in_specs, out_specs=part
        ),
        input_output_aliases=aliases,
        compiler_params=pltpu.CompilerParams(vmem_limit_bytes=VMEM_LIMIT),
        cost_estimate=pl.CostEstimate(
            flops=count * 12 * rows * cols * head_dim * head_dim,
            transcendentals=0,
            bytes_accessed=count * 8 * rows * cols * head_dim,
        ),
    )(base, block, *operands)


def divided(value, by):
    return ((value.astype(jnp.float32) + 0.5) * (1.0 / by)).astype(jnp.int32)


def local_kernel(grid, first, aliased, tile_ref, radii_ref, *refs):
    n_col, n_row = len(grid.col_sides), len(grid.row_sides)
    query_ref, key_ref, value_ref = refs[:3]
    col_in = refs[3 : 3 + n_col]
    row_in = refs[3 + n_col : 3 + n_col + n_row]
    corner_in = refs[3 + n_col + n_row : 3 + n_col + n_row + n_col * n_row]
    out_ref, reach_ref = refs[-2:]
    rows, cols, head_dim = query_ref.shape[2:]
    tokens = rows * cols

    @pl.when(pl.program_id(0) == 0)
    def _():
        row, col = grid.place(tile_ref[0])

        def span(count):
            return lax.broadcasted_iota(jnp.int32, (1, count), 1)

        index = span(tokens)
        key_row = [divided(index, cols)]
        key_col = [index - key_row[0] * cols]
        for side in grid.col_sides:
            after = grid.lies_after(col, side)
            there = grid.exists(col, side, grid.cols)
            index = span(R_MAX * rows)
            step = divided(index, rows)
            place = pick(after, cols + step, -1 - step)
            key_row.append(index - step * rows)
            key_col.append(pick(there, place, -(1 << 20)))
        for side in grid.row_sides:
            after = grid.lies_after(row, side)
            there = grid.exists(row, side, grid.rows)
            index = span(R_MAX * cols)
            step = divided(index, cols)
            place = pick(after, rows + step, -1 - step)
            key_row.append(pick(there, place, -(1 << 20)))
            key_col.append(index - step * cols)
        for row_side in grid.row_sides:
            for col_side in grid.col_sides:
                below = grid.lies_after(row, row_side)
                right = grid.lies_after(col, col_side)
                index = span(R_MAX * R_MAX)
                step = divided(index, R_MAX)
                place = pick(below, rows + step, step - R_MAX)
                there = grid.exists(row, row_side, grid.rows)
                key_row.append(pick(there, place, -(1 << 20)))
                step = index - step * R_MAX
                place = pick(right, cols + step, step - R_MAX)
                there = grid.exists(col, col_side, grid.cols)
                key_col.append(pick(there, place, -(1 << 20)))
        key_row = jnp.concatenate(key_row, axis=1)
        key_col = jnp.concatenate(key_col, axis=1)
        index = lax.broadcasted_iota(jnp.int32, (tokens, 1), 0)
        query_row = divided(index, cols)
        query_col = index - query_row * cols
        reach_ref[...] = jnp.maximum(
            jnp.abs(query_row - key_row), jnp.abs(query_col - key_col)
        )

    def gathered(own, kind):
        parts = [own[0, 0].reshape(tokens, head_dim)]
        parts += [ref[:, kind].reshape(R_MAX * rows, head_dim) for ref in col_in]
        parts += [ref[:, kind].reshape(R_MAX * cols, head_dim) for ref in row_in]
        parts += [ref[kind] for ref in corner_in]
        return jnp.concatenate(parts, axis=0)

    radius = radii_ref[first + pl.program_id(0)]
    query = query_ref[0, 0].reshape(tokens, head_dim)
    scores = lax.dot_general(
        query, gathered(key_ref, 0), (((1,), (1,)), ((), ())), precision=EXACT,
        preferred_element_type=jnp.float32,
    ) / math.sqrt(head_dim)
    scores = jnp.where(reach_ref[...] <= radius, scores, jnp.float32(-1e30))
    top = jnp.max(scores, axis=1, keepdims=True)
    weights = jnp.exp(scores - top)
    total = jnp.sum(weights, axis=1, keepdims=True)
    result = jnp.dot(
        weights, gathered(value_ref, 1), precision=EXACT,
        preferred_element_type=jnp.float32,
    )
    out_ref[0, 0] = (result / total).reshape(rows, cols, head_dim)


def local_part(grid, first, count, tile, radii, queries, keys, values, sides, onto=None):
    rows, cols, dim = queries.shape[2:]
    heads = radii.shape[0]
    head_dim = dim // heads
    part = pl.BlockSpec((1, 1, rows, cols, head_dim), lambda i, *_: (0, 0, 0, 0, first + i))
    col_in, row_in, corner_in = sides
    operands = [queries, keys, values, *col_in, *row_in, *corner_in]
    in_specs = [part] * 3
    for length, group in ((rows, col_in), (cols, row_in)):
        for array in group:
            start = first if array.shape[0] == heads * R_MAX else 0
            in_specs.append(
                pl.BlockSpec(
                    (R_MAX, 2, length, head_dim),
                    lambda i, *_, start=start: (start + i, 0, 0, 0),
                )
            )
    for _ in corner_in:
        in_specs.append(
            pl.BlockSpec((2, R_MAX * R_MAX, head_dim), lambda i, *_: (0, 0, first + i))
        )
    aliases = {}
    if onto is not None:
        aliases = {2 + len(operands): 0}
        operands.append(onto)
        in_specs.append(pl.BlockSpec(memory_space=pl.ANY))
    tokens = rows * cols
    held = (
        tokens
        + R_MAX * (rows * len(col_in) + cols * len(row_in))
        + R_MAX * R_MAX * len(corner_in)
    )
    return pl.pallas_call(
        functools.partial(local_kernel, grid, first, onto is not None),
        name="local_heads",
        out_shape=jax.ShapeDtypeStruct(queries.shape, jnp.float32),
        grid_spec=pltpu.PrefetchScalarGridSpec(
            num_scalar_prefetch=2,
            grid=(count,),
            in_specs=in_specs,
            out_specs=part,
            scratch_shapes=[pltpu.VMEM((tokens, held), jnp.int32)],
        ),
        input_output_aliases=aliases,
        compiler_params=pltpu.CompilerParams(vmem_limit_bytes=VMEM_LIMIT),
        cost_estimate=pl.CostEstimate(
            flops=count * 24 * tokens * held * head_dim,
            transcendentals=count * tokens * held,
            bytes_accessed=count * 16 * tokens * head_dim,
        ),
    )(tile, radii, *operands)


def swapped(value, axis, bit):
    count = lax.axis_size(axis)
    return lax.ppermute(value, axis, [(source, source ^ bit) for source in range(count)])


def bits(count, start=1):
    assert count & (count - 1) == 0
    bit = start
    while bit < count:
        yield bit
        bit *= 2


def body(queries, keys, values, radii):
    rows, cols, dim = queries.shape[2:]
    heads = radii.shape[0]
    grid = Grid(lax.axis_size("tile"), lax.axis_size("block"))
    tile_here = lax.axis_index("tile")
    block_here = lax.axis_index("block")
    tile = tile_here.astype(jnp.int32).reshape(1)
    block = block_here.astype(jnp.int32).reshape(1)

    packed = list(pack(grid, tile, keys, values, heads))
    col_in = [
        lax.ppermute(packed.pop(0), "tile", grid.pairs(None, side)) for side in grid.col_sides
    ]
    row_in = [
        lax.ppermute(packed.pop(0), "tile", grid.pairs(side, None)) for side in grid.row_sides
    ]
    corner_in = [
        lax.ppermute(packed.pop(0), "tile", grid.pairs(row_side, col_side))
        for row_side in grid.row_sides
        for col_side in grid.col_sides
    ]

    half = heads // 2
    odd = tile & 1
    own, other = odd * half, (1 - odd) * half
    sent = states(other, keys, values, heads, half)
    held = states(own, keys, values, heads, half) + swapped(sent, "tile", 1)
    total, before = held, None
    for bit in bits(grid.blocks):
        if 2 * bit < grid.blocks:
            arrived = swapped(total, "block", bit)
            total = total + arrived
            arrived = jnp.where(block_here & bit, arrived, 0.0)
        else:
            arrived = lax.ppermute(total, "block", [(k, k + bit) for k in range(bit)])
        before = arrived if before is None else before + arrived
    if before is not None:
        held = held + before
    for bit in bits(grid.tiles, 2):
        held = held + swapped(held, "tile", bit)
    tokens = grid.tiles * rows * cols
    global_out = global_part(own, block, queries, held, tokens, heads)
    rest = swapped(held, "tile", 1)
    global_out = global_part(other, block, queries, rest, tokens, heads, onto=global_out)

    sides = (col_in, row_in, corner_in)
    local_out = local_part(grid, 0, heads, tile, radii, queries, keys, values, sides)
    return local_out, global_out


def solution(mesh):
    split = P(("groups", "block"), "tile", None, None, None)
    return jax.shard_map(
        body,
        mesh=mesh,
        in_specs=(split, split, split, P()),
        out_specs=(split, split),
        check_vma=False,
    )
```

time: 246 us -> 133 us (0.54); the launches traced: 243 us -> 133 us
  matrix products: 35.6 us -> 0 us
  waiting for transfers between devices: 119 us -> 84.2 us
  local copies, waits for them, and re-layouts: 29.3 us -> 3.69 us
  Pallas kernels: 0 us -> 25.6 us
  blocking collectives: 22.2 us -> 0 us
  other arithmetic: 18.4 us -> 2.56 us
  between operations: 14.2 us -> 0.73 us
  starting transfers between devices: 3.96 us -> 15.8 us
    dot_general x5 -> x0, matrix products: 35.6 us -> none  [the longest x1 14.4 us: neighborhood(): jnp.einsum('hqk,khd->qhd', weights, value_rows, precision=lax.Precision.H...]
    pallas_call x0 -> x6, Pallas kernels: none -> 25.6 us  [the longest x1 18.5 us: local_part(): pl.pallas_call(functools.partial(local_kernel, grid, first, onto is not N...]
    psum x1 -> x0, waiting for transfers between devices: 24.6 us -> none  [body(): full_state, full_z, full_v = lax.psum(add_states(earlier, own), 'tile')]
    another operation x5 -> x0, local copies, waits for them, and re-layouts: 17.1 us -> none  [the longest x1 5.29 us: neighborhood(): value_rows = value_tile.reshape(key_h * key_w, head_count, head_dim)]
    all_gather x2 -> x0, blocking collectives: 12.3 us -> none  [entering(): everything = jax.tree.map(lambda part: lax.all_gather(part, axis), shard)]
    ppermute x4 -> x8, starting transfers between devices: 3.88 us -> 15.8 us  [the longest x4 8.38 us: swapped(): lax.ppermute(value, axis, [(source, source ^ bit) for source in range(cou...]
    ppermute x4 -> x8, waiting for transfers between devices: 94.6 us -> 84.2 us  [the longest x4 64.9 us: swapped(): lax.ppermute(value, axis, [(source, source ^ bit) for source in range(cou...]
    psum x1 -> x0, blocking collectives: 9.89 us -> none  [body(): full_state, full_z, full_v = lax.psum(add_states(earlier, own), 'tile')]
  transfers between devices with their start and end apart: 6 -> 8, of which waited for: 5 -> 5; matrix products, arithmetic and copies ran while one was open for 22% -> 1% of each run, Pallas kernels for 0% -> 17%
where the time goes in v1:
time: 133 us
  waiting for transfers between devices  84.2 us (63%)
  Pallas kernels  25.6 us (19%)
  starting transfers between devices  15.8 us (12%)
  local copies, waits for them, and re-layouts  3.69 us (3%)
  other arithmetic  2.56 us (2%)
    ppermute x4, waiting for transfers between devices, swapped(): lax.ppermute(value, axis, [(source, source ^ bit) for source in range(cou...  64.9 us
    pallas_call x1, Pallas kernels, local_part(): pl.pallas_call(functools.partial(local_kernel, grid, first, onto is not N...  18.5 us
    ppermute x1, waiting for transfers between devices, body(): lax.ppermute(packed.pop(0), 'tile', grid.pairs(None, side))  9.91 us
    ppermute x1, waiting for transfers between devices, body(): arrived = lax.ppermute(total, 'block', [(k, k + bit) for k in range(bit)])  9.4 us
    ppermute x4, starting transfers between devices, swapped(): lax.ppermute(value, axis, [(source, source ^ bit) for source in range(cou...  8.38 us
    ppermute x1, starting transfers between devices, body(): arrived = lax.ppermute(total, 'block', [(k, k + bit) for k in range(bit)])  3.92 us
    unnamed x18, local copies, waits for them, and re-layouts  3.69 us
    pallas_call x2, Pallas kernels, global_part(): pl.pallas_call(functools.partial(global_kernel, tokens, onto is not None)...  3.65 us
  transfers between devices with their start and end apart: 8, of which 5 were waited for; matrix products, arithmetic and copies ran while one was open for 1% of the time, Pallas kernels for 17%

profile of v1, /device:TPU:17, one launch (start us, length us, event | category | flops | bytes accessed | tf_op | source)
XLA Modules:
  0.0 132.7 jit_solution(6903737244048038315)
XLA Ops:
  0.6 0.0 copy-start
  0.6 1.4 %copy-done = f32[1,1,16,24,1024]{4,3,2,1,0:T(8,128)S(1)} copy-done((f32[1,1,16,24,1024]{4,3,2,1,0:T(8,128)S(1)}, f32[1,1,16,24,1024]{4,3,2,1,0:T(8,128)}, u32[]{:S(2)}) %copy-start) | copy-done | bytes 1572888
  2.0 0.0 copy-start.2
  2.0 1.4 %copy-done.2 = f32[1,1,16,24,1024]{4,3,2,1,0:T(8,128)S(1)} copy-done((f32[1,1,16,24,1024]{4,3,2,1,0:T(8,128)S(1)}, f32[1,1,16,24,1024]{4,3,2,1,0:T(8,128)}, u32[]{:S(2)}) %copy-start.2) | copy-done | bytes 1572888
  3.5 1.5 %head_states.3 = f32[2,264,256]{2,1,0:T(8,128)S(1)} custom-call(s32[1]{0:T(128)S(6)} %mul.6.base_ref, f32[1,1,16,24,1024]{4,3,2,1,0:T(8,128)S(1)} %copy-done, f32[1,1,16,24,1024]{4,3,2,1,0:T(8,128)S(1)} %copy-done.2), custom_call_target="tpu_custom_call" | custom-call | flops 603979776 | bytes 1572864 | tf_op jit(solution)/shard_map/head_states/pallas_call | solution.py:194
  5.0 1.4 %collective-permute-start.3 = (f32[2,264,256]{2,1,0:T(8,128)S(1)}, f32[2,264,256]{2,1,0:T(8,128)S(1)}, u32[]{:S(2)}, u32[]{:S(2)}) collective-permute-start(f32[2,264,256]{2,1,0:T(8,128)S(1)} %head_states.3), channel_id=1, source_target_pairs={{0,1},{1,0},{2,3},{3,2},{4,5},{5,4},{6,7},{7,6},{8,9},{9,8},{10,11... | collective-permute-start | bytes 1622024 | tf_op jit(solution)/shard_map/ppermute | solution.py:410
  6.3 1.5 %head_states.2 = f32[2,264,256]{2,1,0:T(8,128)S(1)} custom-call(s32[1]{0:T(128)S(6)} %mul.7.base_ref, f32[1,1,16,24,1024]{4,3,2,1,0:T(8,128)S(1)} %copy-done, f32[1,1,16,24,1024]{4,3,2,1,0:T(8,128)S(1)} %copy-done.2), custom_call_target="tpu_custom_call" | custom-call | flops 603979776 | bytes 1572864 | tf_op jit(solution)/shard_map/head_states/pallas_call | solution.py:194
  7.8 0.0 copy-start.1
  7.8 10.4 %collective-permute-done.3 = f32[2,264,256]{2,1,0:T(8,128)S(1)} collective-permute-done((f32[2,264,256]{2,1,0:T(8,128)S(1)}, f32[2,264,256]{2,1,0:T(8,128)S(1)}, u32[]{:S(2)}, u32[]{:S(2)}) %collective-permute-start.3) | collective-permute-done | bytes 540704 | tf_op jit(solution)/shard_map/ppermute | solution.py:410
  18.2 0.1 add.15
  18.3 0.0 copy-start.7
  18.3 1.6 %collective-permute-start.4 = (f32[2,264,256]{2,1,0:T(8,128)S(1)}, f32[2,264,256]{2,1,0:T(8,128)S(1)}, u32[]{:S(2)}, u32[]{:S(2)}) collective-permute-start(f32[2,264,256]{2,1,0:T(8,128)S(1)} %add.15), channel_id=1, source_target_pairs={{0,4},{4,0},{8,12},{12,8},{1,5},{5,1},{9,13},{13,9},{2,6},{6,2},{1... | collective-permute-start | bytes 1622024 | tf_op jit(solution)/shard_map/ppermute | solution.py:410
  19.9 1.6 %collective-permute-done.4 = f32[2,264,256]{2,1,0:T(8,128)S(1)} collective-permute-done((f32[2,264,256]{2,1,0:T(8,128)S(1)}, f32[2,264,256]{2,1,0:T(8,128)S(1)}, u32[]{:S(2)}, u32[]{:S(2)}) %collective-permute-start.4) | collective-permute-done | bytes 540704 | tf_op jit(solution)/shard_map/ppermute | solution.py:410
  21.4 0.0 copy-start.8
  21.4 0.9 add.16
  22.4 0.0 copy-done.8
  22.4 3.9 %collective-permute-start.5 = (f32[2,264,256]{2,1,0:T(8,128)}, f32[2,264,256]{2,1,0:T(8,128)}, u32[]{:S(2)}, u32[]{:S(2)}) collective-permute-start(f32[2,264,256]{2,1,0:T(8,128)} %add.16), channel_id=1, source_target_pairs={{0,8},{4,12},{1,9},{5,13},{2,10},{6,14},{3,11},{7,15},{16,24},{20,... | collective-permute-start | bytes 1622024 | tf_op jit(solution)/shard_map/ppermute | solution.py:455
  26.3 0.0 copy-done.1
  26.3 0.5 pack_edges.1
  26.8 0.0 copy-done.7
  26.8 0.0 copy-start.5
  26.8 0.8 copy-done.5
  27.6 0.1 collective-permute-start.1
  27.7 0.0 copy-start.3
  27.7 0.0 copy-start.4
  27.7 0.0 copy-start.6
  27.7 9.4 %collective-permute-done.5 = f32[2,264,256]{2,1,0:T(8,128)} collective-permute-done((f32[2,264,256]{2,1,0:T(8,128)}, f32[2,264,256]{2,1,0:T(8,128)}, u32[]{:S(2)}, u32[]{:S(2)}) %collective-permute-start.5) | collective-permute-done | bytes 540704 | tf_op jit(solution)/shard_map/ppermute | solution.py:455
  37.1 1.5 %add_add_fusion = f32[2,264,256]{2,1,0:T(8,128)S(1)} fusion(f32[2,264,256]{2,1,0:T(8,128)} %copy-done.7, f32[2,264,256]{2,1,0:T(8,128)} %collective-permute-done.5, f32[2,264,256]{2,1,0:T(8,128)} %copy-done.8, pred[]{:T(512)S(6)} %ne.4), kind=kLoop, calls=%fused_computation | loop fusion | flops 405504 | bytes 2162689 | tf_op jit(solution)/shard_map/add | solution.py:458
  38.6 0.1 collective-permute-start.6
  38.7 2.4 %collective-permute-start = (f32[16,2,16,256]{3,2,1,0:T(8,128)}, f32[16,2,16,256]{3,2,1,0:T(8,128)S(1)}, u32[]{:S(2)}, u32[]{:S(2)}) collective-permute-start(f32[16,2,16,256]{3,2,1,0:T(8,128)} %copy-done.5), channel_id=1, source_target_pairs={{0,3},{3,0},{2,1},{1,2},{4,7},{7,4},{6,5},{5,6},{8,11},{11,8},{10,... | collective-permute-start | bytes 1572872 | tf_op jit(solution)/shard_map/ppermute | solution.py:432
  41.1 1.1 collective-permute-start.2
  42.2 53.0 %collective-permute-done.6 = f32[2,264,256]{2,1,0:T(8,128)S(1)} collective-permute-done((f32[2,264,256]{2,1,0:T(8,128)S(1)}, f32[2,264,256]{2,1,0:T(8,128)S(1)}, u32[]{:S(2)}, u32[]{:S(2)}) %collective-permute-start.6) | collective-permute-done | bytes 540704 | tf_op jit(solution)/shard_map/ppermute | solution.py:410
  95.2 0.1 add.19.state_ref
  95.3 5.3 %collective-permute-start.7 = (f32[2,264,256]{2,1,0:T(8,128)S(1)}, f32[2,264,256]{2,1,0:T(8,128)S(1)}, u32[]{:S(2)}, u32[]{:S(2)}) collective-permute-start(f32[2,264,256]{2,1,0:T(8,128)S(1)} %add.19.state_ref), channel_id=1, source_target_pairs={{0,1},{1,0},{2,3},{3,2},{4,5},{5,4},{6,7},{7,6},{8,9},{9,8},{10,11... | collective-permute-start | bytes 1622024 | tf_op jit(solution)/shard_map/ppermute | solution.py:410
  100.6 0.0 collective-permute-done.2.refs_5_
  100.6 9.9 %collective-permute-done.refs_3_ = f32[16,2,16,256]{3,2,1,0:T(8,128)S(1)} collective-permute-done((f32[16,2,16,256]{3,2,1,0:T(8,128)}, f32[16,2,16,256]{3,2,1,0:T(8,128)S(1)}, u32[]{:S(2)}, u32[]{:S(2)}) %collective-permute-start) | collective-permute-done | bytes 524320 | tf_op jit(solution)/shard_map/ppermute | solution.py:432
  110.5 0.0 collective-permute-done.1.refs_4_
  110.5 0.0 copy-done.3
  110.5 0.0 copy-done.4
  110.5 0.0 copy-done.6
  110.5 18.5 %local_heads.1 = f32[1,1,16,24,1024]{4,3,2,1,0:T(8,128)} custom-call(s32[1]{0:T(128)} %bitcast.tile_ref, s32[4]{0:T(128)S(1)} %copy-done.6, f32[1,1,16,24,1024]{4,3,2,1,0:T(8,128)S(1)} %copy-done.4, f32[1,1,16,24,1024]{4,3,2,1,0:T(8,128)S(1)} %copy-done.1, f32[1,1,16,24,1024]{4,3,2,1,0:T(8,128)S(1)} %copy-done.3, ...), custom_call_target="tpu_custom_call" | custom-call | flops 5284823040 | bytes 6291456 | tf_op jit(solution)/shard_map/local_heads/pallas_call | solution.py:387
  129.0 1.8 %global_heads.2.refs_0_ = f32[1,1,16,24,1024]{4,3,2,1,0:T(8,128)} custom-call(s32[1]{0:T(128)S(6)} %mul.7.base_ref, s32[1]{0:T(128)} %bitcast.1.block_ref, f32[1,1,16,24,1024]{4,3,2,1,0:T(8,128)S(1)} %copy-done.4, f32[2,264,256]{2,1,0:T(8,128)S(1)} %add.19.state_ref), custom_call_target="tpu_custom_call" | custom-call | flops 603979776 | bytes 1572864 | tf_op jit(solution)/shard_map/global_heads/pallas_call | solution.py:252
  130.9 0.0 collective-permute-done.7.state_ref
  130.9 1.8 %global_heads.3 = f32[1,1,16,24,1024]{4,3,2,1,0:T(8,128)} custom-call(s32[1]{0:T(128)S(6)} %mul.6.base_ref, s32[1]{0:T(128)} %bitcast.1.block_ref, f32[1,1,16,24,1024]{4,3,2,1,0:T(8,128)S(1)} %copy-done.4, f32[2,264,256]{2,1,0:T(8,128)S(1)} %collective-permute-done.7.state_ref, ...), custom_call_target="tpu_custom_call", output_to_operand_aliasing={{}: (4, {})} | custom-call | flops 603979776 | bytes 1572864 | tf_op jit(solution)/shard_map/global_heads/pallas_call | solution.py:252
Async XLA Ops:
  0.6 1.4 %copy-start = (f32[1,1,16,24,1024]{4,3,2,1,0:T(8,128)S(1)}, f32[1,1,16,24,1024]{4,3,2,1,0:T(8,128)}, u32[]{:S(2)}) copy-start(f32[1,1,16,24,1024]{4,3,2,1,0:T(8,128)} %key_ref.3) | copy-start | bytes 4718596
  2.0 1.4 %copy-start.2 = (f32[1,1,16,24,1024]{4,3,2,1,0:T(8,128)S(1)}, f32[1,1,16,24,1024]{4,3,2,1,0:T(8,128)}, u32[]{:S(2)}) copy-start(f32[1,1,16,24,1024]{4,3,2,1,0:T(8,128)} %value_ref.3) | copy-start | bytes 4718596
  5.0 13.2 %collective-permute-start.3 = (f32[2,264,256]{2,1,0:T(8,128)S(1)}, f32[2,264,256]{2,1,0:T(8,128)S(1)}, u32[]{:S(2)}, u32[]{:S(2)}) collective-permute-start(f32[2,264,256]{2,1,0:T(8,128)S(1)} %head_states.3), channel_id=1, source_target_pairs={{0,1},{1,0},{2,3},{3,2},{4,5},{5,4},{6,7},{7,6},{8,9},{9,8},{10,11... | collective-permute-start | bytes 1622024 | tf_op jit(solution)/shard_map/ppermute | solution.py:410
  7.8 18.5 %copy-start.1 = (f32[1,1,16,24,1024]{4,3,2,1,0:T(8,128)S(1)}, f32[1,1,16,24,1024]{4,3,2,1,0:T(8,128)}, u32[]{:S(2)}) copy-start(f32[1,1,16,24,1024]{4,3,2,1,0:T(8,128)} %key_ref.3) | copy-start | bytes 4718596
  18.3 8.5 %copy-start.7 = (f32[2,264,256]{2,1,0:T(8,128)}, f32[2,264,256]{2,1,0:T(8,128)S(1)}, u32[]{:S(2)}) copy-start(f32[2,264,256]{2,1,0:T(8,128)S(1)} %add.15) | copy-start | bytes 1622020
  18.3 3.2 %collective-permute-start.4 = (f32[2,264,256]{2,1,0:T(8,128)S(1)}, f32[2,264,256]{2,1,0:T(8,128)S(1)}, u32[]{:S(2)}, u32[]{:S(2)}) collective-permute-start(f32[2,264,256]{2,1,0:T(8,128)S(1)} %add.15), channel_id=1, source_target_pairs={{0,4},{4,0},{8,12},{12,8},{1,5},{5,1},{9,13},{13,9},{2,6},{6,2},{1... | collective-permute-start | bytes 1622024 | tf_op jit(solution)/shard_map/ppermute | solution.py:410
  21.4 1.0 copy-start.8
  22.4 14.7 %collective-permute-start.5 = (f32[2,264,256]{2,1,0:T(8,128)}, f32[2,264,256]{2,1,0:T(8,128)}, u32[]{:S(2)}, u32[]{:S(2)}) collective-permute-start(f32[2,264,256]{2,1,0:T(8,128)} %add.16), channel_id=1, source_target_pairs={{0,8},{4,12},{1,9},{5,13},{2,10},{6,14},{3,11},{7,15},{16,24},{20,... | collective-permute-start | bytes 1622024 | tf_op jit(solution)/shard_map/ppermute | solution.py:455
  26.8 0.8 copy-start.5
  27.6 82.9 %collective-permute-start.1 = (f32[16,2,24,256]{3,2,1,0:T(8,128)S(1)}, f32[16,2,24,256]{3,2,1,0:T(8,128)S(1)}, u32[]{:S(2)}, u32[]{:S(2)}) collective-permute-start(f32[16,2,24,256]{3,2,1,0:T(8,128)S(1)} %get-tuple-element.6), channel_id=1, source_target_pairs={{1,3},{2,0},{3,1},{0,2},{5,7},{6,4},{7,5},{4,6},{9,11},{10,8},{11,... | collective-permute-start | bytes 2359304 | tf_op jit(solution)/shard_map/ppermute | solution.py:435
  27.7 82.8 %copy-start.3 = (f32[1,1,16,24,1024]{4,3,2,1,0:T(8,128)S(1)}, f32[1,1,16,24,1024]{4,3,2,1,0:T(8,128)}, u32[]{:S(2)}) copy-start(f32[1,1,16,24,1024]{4,3,2,1,0:T(8,128)} %value_ref.3) | copy-start | bytes 4718596
  27.7 82.8 %copy-start.4 = (f32[1,1,16,24,1024]{4,3,2,1,0:T(8,128)S(1)}, f32[1,1,16,24,1024]{4,3,2,1,0:T(8,128)}, u32[]{:S(2)}) copy-start(f32[1,1,16,24,1024]{4,3,2,1,0:T(8,128)} %query_ref.3) | copy-start | bytes 4718596
  27.7 82.8 %copy-start.6 = (s32[4]{0:T(128)S(1)}, s32[4]{0:T(128)}, u32[]{:S(2)}) copy-start(s32[4]{0:T(128)} %radii_ref.1) | copy-start | bytes 52
  38.6 56.6 %collective-permute-start.6 = (f32[2,264,256]{2,1,0:T(8,128)S(1)}, f32[2,264,256]{2,1,0:T(8,128)S(1)}, u32[]{:S(2)}, u32[]{:S(2)}) collective-permute-start(f32[2,264,256]{2,1,0:T(8,128)S(1)} %add_add_fusion), channel_id=1, source_target_pairs={{0,2},{1,3},{2,0},{3,1},{4,6},{5,7},{6,4},{7,5},{8,10},{9,11},{10,... | collective-permute-start | bytes 1622024 | tf_op jit(solution)/shard_map/ppermute | solution.py:410
  38.7 71.8 %collective-permute-start = (f32[16,2,16,256]{3,2,1,0:T(8,128)}, f32[16,2,16,256]{3,2,1,0:T(8,128)S(1)}, u32[]{:S(2)}, u32[]{:S(2)}) collective-permute-start(f32[16,2,16,256]{3,2,1,0:T(8,128)} %copy-done.5), channel_id=1, source_target_pairs={{0,3},{3,0},{2,1},{1,2},{4,7},{7,4},{6,5},{5,6},{8,11},{11,8},{10,... | collective-permute-start | bytes 1572872 | tf_op jit(solution)/shard_map/ppermute | solution.py:432
  41.1 59.5 %collective-permute-start.2 = (f32[2,16,1024]{2,1,0:T(8,128)S(1)}, f32[2,16,1024]{2,1,0:T(8,128)S(1)}, u32[]{:S(2)}, u32[]{:S(2)}) collective-permute-start(f32[2,16,1024]{2,1,0:T(8,128)S(1)} %get-tuple-element.7), channel_id=1, source_target_pairs={{2,3},{1,0},{0,1},{3,2},{6,7},{5,4},{4,5},{7,6},{10,11},{9,8},{8,9... | collective-permute-start | bytes 393224 | tf_op jit(solution)/shard_map/ppermute | solution.py:438
  95.3 35.6 %collective-permute-start.7 = (f32[2,264,256]{2,1,0:T(8,128)S(1)}, f32[2,264,256]{2,1,0:T(8,128)S(1)}, u32[]{:S(2)}, u32[]{:S(2)}) collective-permute-start(f32[2,264,256]{2,1,0:T(8,128)S(1)} %add.19.state_ref), channel_id=1, source_target_pairs={{0,1},{1,0},{2,3},{3,2},{4,5},{5,4},{6,7},{7,6},{8,9},{9,8},{10,11... | collective-permute-start | bytes 1622024 | tf_op jit(solution)/shard_map/ppermute | solution.py:410
